TPU v7x, 128 devices: a whole 4x4x4 slice. The times are simulated.
128 devices in a mesh: dp: 32 (over z, x, core), mp: 4 (over y).
Axes of the slice: x: 4, y: 4, z: 4, core: 2. Of those that a mesh axis runs over, the one named last changes fastest.
Arguments:
- hidden: bfloat16 [40960, 8192], P('dp', 'mp'), may hold values from -6 to 6
- rewards: float32 [256, 160], P('dp'), may hold values from -4 to 4
- lengths: int32 [256], P('dp'), may hold values from 1 to 160, as said below
- dest_shard: int32 [256], P('dp'), may hold values from 0 to 31, as said below
- source_owner: int32 [256], P('dp'), may hold values from 0 to 31, as said below
- pack_offset: int32 [256], P('dp'), may hold values from 0 to 639, as said below
- segment_ids: int32 [20480], P('dp'), may hold values from 0 to 7, as said below
- norm_gain: float32 [8192], replicated, may hold values from 0.5 to 1.5
- w_query: bfloat16 [8192, 4096], P(None, 'mp'), may hold values from -1 to 1
- w_key: bfloat16 [8192, 512], P(None, 'mp'), may hold values from -1 to 1
- w_value: bfloat16 [8192, 512], P(None, 'mp'), may hold values from -0.0625 to 0.0625
- value_head: float32 [8192], P('mp'), may hold values from -0.0625 to 0.0625
- folded_head: float32 [4096], P('mp'), may hold values from -0.09375 to 0.09375
Outputs:
- values: float32 [256, 160], P('dp')
- advantages: float32 [256, 160], P('dp')
Inputs may be any that keep to these rules, and one draw needn't show every extreme that they name: `lengths`: rows of a slot past its rollout's length are unused. Every critic shard holds a rollout of 160 rows. Some owner's 8 rollouts all have 160 rows. `dest_shard`: owner o packs its 8 rollouts on the shards o, o + 1, ..., o + 7, modulo the number of shards, one on each. `source_owner`: shard s packs one rollout from each of the owners s, s - 1, ..., s - 7, modulo the number of shards, in some order, agreeing with dest_shard. `pack_offset`: A shard's packed rollouts lie back to back in the order of their index, each with the length that lengths gives it, and fill all 640 rows. `segment_ids`: each packed row names the index of the packed rollout that holds it, as pack_offset and lengths lay them out.
All inputs are finite; a program needn't handle non-finite values.
Results may differ from a plain program's by a relative error of at most 0.007.
Values may be sent and summed in bfloat16 or wider, within the bound.
A program may use at most 192 MiB of HBM per device.

v0:
```python
import math
import jax
import jax.numpy as jnp
from jax import lax
from jax.sharding import PartitionSpec as P

HD = 128
EPSILON = 1e-05
DISCOUNT = 0.99
SMOOTHING = 0.95
ROPE_BASE = 500000.0


def passed_along(value, axis, by):
    length = lax.axis_size(axis)
    return lax.ppermute(value, axis, [(i, (i + by) % length) for i in range(length)])


def rotary(values_in, positions):
    half_width = values_in.shape[-1] // 2
    frequency = ROPE_BASE ** (-jnp.arange(half_width, dtype=jnp.float32) / half_width)
    angles = positions.astype(jnp.float32)[:, None] * frequency[None, :]
    cosine = jnp.cos(angles)[:, None, :]
    sine_part = jnp.sin(angles)[:, None, :]
    front_half = values_in[..., :half_width]
    back_half = values_in[..., half_width:]
    return jnp.concatenate(
        [front_half * cosine - back_half * sine_part, back_half * cosine + front_half * sine_part],
        axis=-1,
    )


def head_values(queries, keys_out, values_out, segments, positions, folded_head):
    row_count = queries.shape[0]
    kv_count = keys_out.shape[1] // HD
    group_size = queries.shape[1] // HD // kv_count
    query_rot = rotary(queries.reshape(row_count, kv_count * group_size, HD), positions).astype(
        jnp.bfloat16
    )
    query_rot = query_rot.reshape(row_count, kv_count, group_size, HD)
    key_rot = rotary(keys_out.reshape(row_count, kv_count, HD), positions).astype(jnp.bfloat16)
    value_rows = values_out.astype(jnp.bfloat16).reshape(row_count, kv_count, HD)
    scores = jnp.einsum(
        "qhgd,khd->hgqk", query_rot, key_rot, preferred_element_type=jnp.float32
    ) / math.sqrt(HD)
    allowed = (segments[:, None] == segments[None, :]) & (positions[:, None] >= positions[None, :])
    scores = jnp.where(allowed[None, None], scores, -1e30)
    row_max = jnp.max(scores, axis=-1, keepdims=True)
    exp_scores = jnp.where(allowed[None, None], jnp.exp(scores - row_max), 0.0)
    row_total = jnp.sum(exp_scores, axis=-1, keepdims=True)
    weights = (exp_scores / row_total).astype(jnp.bfloat16)
    attended = jnp.einsum("hgqk,khd->qhgd", weights, value_rows, preferred_element_type=jnp.float32)
    return jnp.sum(attended.reshape(row_count, -1) * folded_head[None, :], axis=1)


def local(
    hidden,
    rewards,
    lengths,
    dest_shard,
    source_owner,
    pack_offset,
    segment_ids,
    norm_gain,
    w_query,
    w_key,
    w_value,
    value_head,
    folded_head,
):
    shards = lax.axis_size("dp")
    shard_index = lax.axis_index("dp")
    rollouts = lengths.shape[0]
    slot_rows = rewards.shape[1]
    packed_rows = segment_ids.shape[0]
    part_width = hidden.shape[1]
    slot_lanes = jnp.arange(rollouts, dtype=jnp.int32)

    def slot_for(shift_by):
        target = (shard_index + shift_by) % shards
        return jnp.sum(jnp.where(dest_shard == target, slot_lanes, 0))

    def outgoing(shift_by, source):
        return lax.dynamic_slice_in_dim(source, slot_for(shift_by) * slot_rows, slot_rows, 0)

    source_step = (shard_index - source_owner) % shards
    lane_match = segment_ids[:, None] == slot_lanes[None, :]
    row_step = jnp.sum(jnp.where(lane_match, source_step[None, :], 0), axis=1)
    row_offset = jnp.sum(jnp.where(lane_match, pack_offset[None, :], 0), axis=1)
    positions = jnp.arange(packed_rows, dtype=jnp.int32) - row_offset
    pick_rows = row_step * slot_rows + positions
    full_rows = lax.all_gather(hidden, "mp", axis=1, tiled=True)
    received = [outgoing(0, full_rows)]
    for shift_by in range(1, rollouts):
        received.append(passed_along(outgoing(shift_by, full_rows), "dp", shift_by))
    packed = jnp.take(jnp.concatenate(received, axis=0), pick_rows, axis=0)
    packed_f = packed.astype(jnp.float32)
    row_scale = lax.rsqrt(jnp.mean(packed_f * packed_f, axis=1) + EPSILON)
    normed = (packed_f * row_scale[:, None] * norm_gain[None, :]).astype(jnp.bfloat16)
    queries = jnp.dot(normed, w_query, preferred_element_type=jnp.float32)
    keys_out = jnp.dot(normed, w_key, preferred_element_type=jnp.float32)
    values_out = jnp.dot(normed, w_value, preferred_element_type=jnp.float32)
    own_part = lax.dynamic_slice_in_dim(packed, lax.axis_index("mp") * part_width, part_width, 1)
    value_terms = head_values(queries, keys_out, values_out, segment_ids, positions, folded_head)
    value_terms = value_terms + jnp.sum(own_part.astype(jnp.float32) * value_head[None, :], axis=1)
    packed_values = lax.psum(value_terms, "mp")
    padded = jnp.concatenate([packed_values, jnp.zeros((slot_rows,), jnp.float32)])
    slot_values = jnp.zeros((rollouts, slot_rows), jnp.float32)
    for shift_by in range(rollouts):
        owner_now = (shard_index - shift_by) % shards
        j_index = jnp.sum(jnp.where(source_owner == owner_now, slot_lanes, 0))
        start_at = jnp.sum(jnp.where(slot_lanes == j_index, pack_offset, 0))
        arrived = lax.dynamic_slice_in_dim(padded, start_at, slot_rows, 0)
        if shift_by:
            arrived = passed_along(arrived, "dp", -shift_by)
        slot_values = jnp.where(
            (slot_lanes == slot_for(shift_by))[:, None], arrived[None, :], slot_values
        )
    step_ids = jnp.arange(slot_rows, dtype=jnp.int32)
    live_mask = step_ids[None, :] < lengths[:, None]
    values = jnp.where(live_mask, slot_values, 0.0)
    next_live = step_ids[None, :] + 1 < lengths[:, None]
    following = jnp.concatenate([values[:, 1:], jnp.zeros((rollouts, 1), jnp.float32)], axis=1)
    one_step = jnp.where(
        live_mask, rewards + DISCOUNT * jnp.where(next_live, following, 0.0) - values, 0.0
    )
    lag_matrix = (step_ids[:, None] - step_ids[None, :]).astype(jnp.float32)
    decay_table = jnp.where(
        lag_matrix >= 0, jnp.exp(lag_matrix * math.log(DISCOUNT * SMOOTHING)), 0.0
    )
    advantages = jnp.dot(one_step, decay_table, precision=lax.Precision.HIGHEST)
    return (values, advantages)


def solution(mesh):
    return jax.shard_map(
        local,
        mesh=mesh,
        in_specs=(
            P("dp", "mp"),
            P("dp", None),
            P("dp"),
            P("dp"),
            P("dp"),
            P("dp"),
            P("dp"),
            P(),
            P(None, "mp"),
            P(None, "mp"),
            P(None, "mp"),
            P("mp"),
            P("mp"),
        ),
        out_specs=(P("dp", None), P("dp", None)),
        check_vma=False,
    )
```

profile of v0, /device:TPU:1, one launch (start us, length us, event | category | flops | bytes accessed | tf_op | source)
XLA Modules:
  0.0 709.8 jit_solution(8402809665676939686)
XLA Ops:
  7.2 0.7 all-gather.2.cloned.1.call-update
  8.1 1.7 fusion.49
  15.0 187.3 %all-gather.2.cloned.1.call-done = bf16[1280,8192]{1,0:T(8,128)(2,1)} async-done(((bf16[1280,2048]{1,0:T(8,128)(2,1)}), bf16[1280,8192]{1,0:T(8,128)(2,1)}) %all-gather.2.cloned.1.call-update) | async-done | bytes 20971536 | tf_op jit(solution)/shard_map/all_gather | solution.py:92
  202.3 14.7 %constant_dynamic-slice_fusion = (bf16[160,8192]{1,0:T(8,128)(2,1)}, bf16[160,8192]{1,0:T(8,128)(2,1)}, bf16[160,8192]{1,0:T(8,128)(2,1)}, bf16[160,8192]{1,0:T(...) fusion(bf16[1280,8192]{1,0:T(8,128)(2,1)} %all-gather.2.cloned., ...), kind=kLoop, calls=%fused_computation.95 | loop fusion | bytes 41943072 | tf_op jit(solution)/shard_map/dynamic_slice | solution.py:84
  217.0 2.0 collective-permute-start
  219.0 5.7 fusion.58
  239.8 0.7 iota_compare_fusion.10
  240.5 1.3 collective-permute-start.1
  241.7 0.7 iota_compare_fusion.3
  243.0 0.7 iota_compare_fusion.5
  243.7 0.6 iota_compare_fusion.6
  244.4 0.7 iota_compare_fusion.7
  245.0 1.6 collective-permute-start.2
  247.0 1.2 multiply_cosine_fusion
  248.3 1.6 collective-permute-start.3
  249.9 3.0 collective-permute-start.4
  252.9 0.9 collective-permute-done
  253.8 2.5 collective-permute-start.5
  256.3 3.5 constant_dynamic-update-slice_fusion.6
  259.8 54.1 %collective-permute-done.1 = bf16[160,8192]{1,0:T(8,128)(2,1)S(1)} collective-permute-done((bf16[160,8192]{1,0:T(8,128)(2,1)}, bf16[160,8192]{1,0:T(8,128)(2,1)S(1)}, u32[]{:S(2)}, u32[]{:S(2)}) %collective-permute-start.1) | collective-permute-done | bytes 2621472 | tf_op jit(solution)/shard_map/ppermute | solution.py:16
  313.9 1.7 constant_dynamic-update-slice_fusion.5
  315.7 50.5 %collective-permute-done.2 = bf16[160,8192]{1,0:T(8,128)(2,1)S(1)} collective-permute-done((bf16[160,8192]{1,0:T(8,128)(2,1)}, bf16[160,8192]{1,0:T(8,128)(2,1)S(1)}, u32[]{:S(2)}, u32[]{:S(2)}) %collective-permute-start.2) | collective-permute-done | bytes 2621472 | tf_op jit(solution)/shard_map/ppermute | solution.py:16
  366.2 1.8 constant_dynamic-update-slice_fusion.4
  368.0 99.9 %collective-permute-done.3 = bf16[160,8192]{1,0:T(8,128)(2,1)S(1)} collective-permute-done((bf16[160,8192]{1,0:T(8,128)(2,1)}, bf16[160,8192]{1,0:T(8,128)(2,1)S(1)}, u32[]{:S(2)}, u32[]{:S(2)}) %collective-permute-start.3) | collective-permute-done | bytes 2621472 | tf_op jit(solution)/shard_map/ppermute | solution.py:16
  467.9 1.7 constant_dynamic-update-slice_fusion.3
  469.6 33.6 %collective-permute-done.4 = bf16[160,8192]{1,0:T(8,128)(2,1)S(1)} collective-permute-done((bf16[160,8192]{1,0:T(8,128)(2,1)}, bf16[160,8192]{1,0:T(8,128)(2,1)S(1)}, u32[]{:S(2)}, u32[]{:S(2)}) %collective-permute-start.4) | collective-permute-done | bytes 2621472 | tf_op jit(solution)/shard_map/ppermute | solution.py:16
  503.2 1.7 constant_dynamic-update-slice_fusion.2
  504.9 51.4 %collective-permute-done.5 = bf16[160,8192]{1,0:T(8,128)(2,1)S(1)} collective-permute-done((bf16[160,8192]{1,0:T(8,128)(2,1)}, bf16[160,8192]{1,0:T(8,128)(2,1)S(1)}, u32[]{:S(2)}, u32[]{:S(2)}) %collective-permute-start.5) | collective-permute-done | bytes 2621472 | tf_op jit(solution)/shard_map/ppermute | solution.py:16
  556.3 1.7 constant_dynamic-update-slice_fusion.1
  558.0 29.1 %collective-permute-done.6 = bf16[160,8192]{1,0:T(8,128)(2,1)S(1)} collective-permute-done((bf16[160,8192]{1,0:T(8,128)(2,1)}, bf16[160,8192]{1,0:T(8,128)(2,1)S(1)}, u32[]{:S(2)}, u32[]{:S(2)}) %collective-permute-start.6) | collective-permute-done | bytes 2621472 | tf_op jit(solution)/shard_map/ppermute | solution.py:16
  587.2 1.7 constant_dynamic-update-slice_fusion
  588.8 31.5 %gather_fusion = bf16[640,8192]{1,0:T(8,128)(2,1)} fusion(bf16[1280,8192]{1,0:T(8,128)(2,1)} %constant_dynamic-update-slice_fusion, s32[1024]{0:T(1024)S(1)} %pad_clamp_fusion), kind=kCustom, calls=%fused_computation | custom fusion | bytes 20974080 | tf_op jit(solution)/shard_map/jit(_take)/gather | solution.py:96
  620.3 7.7 %fusion = (f32[640]{0:T(1024)S(1)}, bf16[640,8192]{1,0:T(8,128)(2,1)S(1)}) fusion(bf16[640,8192]{1,0:T(8,128)(2,1)} %gather_fusion, pred[640]{0:T(1024)(128)(4,1)S(1)} %compare_and_fusion.1), kind=kLoop, calls=%fused_computation.3 | loop fusion | flops 20970880 | bytes 20974720 | tf_op jit(solution)/shard_map/reduce_sum | solution.py:98
  628.0 3.3 convolution_bitcast_fusion.1
  631.3 0.7 fusion.36
  632.0 14.4 %convolution_bitcast_fusion = f32[80,8,8,128]{3,1,2,0:T(8,128)S(1)} fusion(bf16[8192,1024]{1,0:T(8,128)(2,1)} %param.21, bf16[640,8192]{1,0:T(8,128)(2,1)S(1)} %get-tuple-element.29, f32[8192]{0:T(1024)S(1)} %copy-done.8, f32[640]{0:T(1024)S(1)} %add_rsqrt_fusion), kind=kOutput, calls=%fused_computation.20 | convolution fusion | flops 10758389760 | bytes 29919744 | tf_op jit(solution)/shard_map/dot_general | solution.py:100
  647.0 0.8 fusion.86
  647.9 1.0 subtract_convert_fusion
  648.9 6.4 fusion.3
  655.3 7.8 %fusion.4 = f32[8,640]{1,0:T(8,128)S(1)} fusion(f32[640,640,8]{1,0,2:T(8,128)} %get-tuple-element.58, f32[8,640]{1,0:T(8,128)S(1)} %get-tuple-element.57, pred[640,640]{0,1:T(8,128)(4,1)S(1)} %compare_and_fusion), kind=kLoop, calls=%fused_computation.11 | loop fusion | flops 16378880 | bytes 13557760 | tf_op jit(solution)/shard_map/reduce_sum | solution.py:50
  663.8 14.8 %fusion.7 = f32[640]{0:T(1024)S(1)} fusion(f32[8,640]{1,0:T(8,128)S(1)} %fusion.4, f32[8,640]{1,0:T(8,128)S(1)} %get-tuple-element.57, f32[640,640,8]{1,0,2:T(8,128)} %get-tuple-element.58, pred[640,640]{0,1:T(8,128)(4,1)S(1)} %compare_and_fusion, f32[8,128]{1,0:T(8,128)S(1)} %bitcast.51, bf16[8192,128]{1,0:T(8,128)(2,1)} %param.23, ...), kind=kOutput, calls=%fused_computation.16 | convolution fusion | flops 2223062528 | bytes 26182656 | tf_op jit(solution)/shard_map/hgqk,khd->qhgd/dot_general | solution.py:52
  678.6 6.7 psum.7
  685.6 0.6 iota_compare_fusion.8
  686.2 9.0 %collective-permute-start.12 = (f32[160]{0:T(256)S(1)}, f32[160]{0:T(256)S(1)}, u32[]{:S(2)}, u32[]{:S(2)}) collective-permute-start(f32[160]{0:T(256)S(1)} %get-tuple-element.51), channel_id=1, source_target_pairs={{0,120},{4,124},{8,0},{12,4},{16,8},{20,12},{24,16},{28,20},{32,24... | collective-permute-start | bytes 1928 | tf_op jit(solution)/shard_map/ppermute | solution.py:16
  695.2 1.9 collective-permute-start.7
  698.4 2.4 collective-permute-done.8
  700.8 0.9 collective-permute-done.9
  701.9 0.8 fusion.25
  (52 shorter events, 4.0 us)
Async XLA Ops:
  7.2 620.9 %copy-start = (bf16[8192,128]{1,0:T(8,128)(2,1)S(1)}, bf16[8192,128]{1,0:T(8,128)(2,1)}, u32[]{:S(2)}) copy-start(bf16[8192,128]{1,0:T(8,128)(2,1)} %param.22) | copy-start | bytes 6291460
  7.2 195.1 %all-gather.2.cloned.1.call-start = ((), (), s32[]{:S(2)}) async-start(), calls=%async_computation | async-start | bytes 26214400 | tf_op jit(solution)/shard_map/all_gather | solution.py:92
  14.9 204.1 %copy-start.6 = (s32[8]{0:T(128)S(1)}, s32[8]{0:T(128)}, u32[]{:S(2)}) copy-start(s32[8]{0:T(128)} %param.18) | copy-start | bytes 100
  15.0 224.7 %copy-start.3 = (s32[640]{0:T(1024)S(1)}, s32[640]{0:T(1024)}, u32[]{:S(2)}) copy-start(s32[640]{0:T(1024)} %param.19) | copy-start | bytes 7684
  217.0 36.8 %collective-permute-start = (bf16[160,8192]{1,0:T(8,128)(2,1)}, bf16[160,8192]{1,0:T(8,128)(2,1)}, u32[]{:S(2)}, u32[]{:S(2)}) collective-permute-start(bf16[160,8192]{1,0:T(8,128)(2,1)} %get-tuple-element.36), channel_id=1, source_target_pairs={{0,4},{4,8},{8,12},{12,16},{16,20},{20,24},{24,28},{28,32},{32,36}... | collective-permute-start | bytes 7864328 | tf_op jit(solution)/shard_map/ppermute | solution.py:16
  240.5 73.5 %collective-permute-start.1 = (bf16[160,8192]{1,0:T(8,128)(2,1)}, bf16[160,8192]{1,0:T(8,128)(2,1)S(1)}, u32[]{:S(2)}, u32[]{:S(2)}) collective-permute-start(bf16[160,8192]{1,0:T(8,128)(2,1)} %get-tuple-element.35), channel_id=1, source_target_pairs={{0,8},{4,12},{8,16},{12,20},{16,24},{20,28},{24,32},{28,36},{32,40... | collective-permute-start | bytes 7864328 | tf_op jit(solution)/shard_map/ppermute | solution.py:16
  245.0 121.1 %collective-permute-start.2 = (bf16[160,8192]{1,0:T(8,128)(2,1)}, bf16[160,8192]{1,0:T(8,128)(2,1)S(1)}, u32[]{:S(2)}, u32[]{:S(2)}) collective-permute-start(bf16[160,8192]{1,0:T(8,128)(2,1)} %get-tuple-element.34), channel_id=1, source_target_pairs={{0,12},{4,16},{8,20},{12,24},{16,28},{20,32},{24,36},{28,40},{32,4... | collective-permute-start | bytes 7864328 | tf_op jit(solution)/shard_map/ppermute | solution.py:16
  248.3 219.6 %collective-permute-start.3 = (bf16[160,8192]{1,0:T(8,128)(2,1)}, bf16[160,8192]{1,0:T(8,128)(2,1)S(1)}, u32[]{:S(2)}, u32[]{:S(2)}) collective-permute-start(bf16[160,8192]{1,0:T(8,128)(2,1)} %get-tuple-element.33), channel_id=1, source_target_pairs={{0,16},{4,20},{8,24},{12,28},{16,32},{20,36},{24,40},{28,44},{32,4... | collective-permute-start | bytes 7864328 | tf_op jit(solution)/shard_map/ppermute | solution.py:16
  249.9 253.3 %collective-permute-start.4 = (bf16[160,8192]{1,0:T(8,128)(2,1)}, bf16[160,8192]{1,0:T(8,128)(2,1)S(1)}, u32[]{:S(2)}, u32[]{:S(2)}) collective-permute-start(bf16[160,8192]{1,0:T(8,128)(2,1)} %get-tuple-element.32), channel_id=1, source_target_pairs={{0,20},{4,24},{8,28},{12,32},{16,36},{20,40},{24,44},{28,48},{32,5... | collective-permute-start | bytes 7864328 | tf_op jit(solution)/shard_map/ppermute | solution.py:16
  253.8 302.5 %collective-permute-start.5 = (bf16[160,8192]{1,0:T(8,128)(2,1)}, bf16[160,8192]{1,0:T(8,128)(2,1)S(1)}, u32[]{:S(2)}, u32[]{:S(2)}) collective-permute-start(bf16[160,8192]{1,0:T(8,128)(2,1)} %get-tuple-element.31), channel_id=1, source_target_pairs={{0,24},{4,28},{8,32},{12,36},{16,40},{20,44},{24,48},{28,52},{32,5... | collective-permute-start | bytes 7864328 | tf_op jit(solution)/shard_map/ppermute | solution.py:16
  313.9 273.2 %collective-permute-start.6 = (bf16[160,8192]{1,0:T(8,128)(2,1)}, bf16[160,8192]{1,0:T(8,128)(2,1)S(1)}, u32[]{:S(2)}, u32[]{:S(2)}) collective-permute-start(bf16[160,8192]{1,0:T(8,128)(2,1)} %get-tuple-element.30), channel_id=1, source_target_pairs={{0,28},{4,32},{8,36},{12,40},{16,44},{20,48},{24,52},{28,56},{32,6... | collective-permute-start | bytes 7864328 | tf_op jit(solution)/shard_map/ppermute | solution.py:16
  620.3 7.7 %copy-start.8 = (f32[8192]{0:T(1024)S(1)}, f32[8192]{0:T(1024)}, u32[]{:S(2)}) copy-start(f32[8192]{0:T(1024)} %param.20) | copy-start | bytes 98308
  628.0 35.1 %copy-start.2 = (bf16[640,8192]{1,0:T(8,128)(2,1)}, bf16[640,8192]{1,0:T(8,128)(2,1)S(1)}, u32[]{:S(2)}) copy-start(bf16[640,8192]{1,0:T(8,128)(2,1)S(1)} %get-tuple-element.29) | copy-start | bytes 31457284
  655.3 7.9 %copy-start.5 = (f32[2048]{0:T(1024)S(1)}, f32[2048]{0:T(1024)}, u32[]{:S(2)}) copy-start(f32[2048]{0:T(1024)} %param.24) | copy-start | bytes 24580
  655.3 8.5 %copy-start.10 = (f32[1024]{0:T(1024)S(1)}, f32[1024]{0:T(1024)}, u32[]{:S(2)}) copy-start(f32[1024]{0:T(1024)} %param.25) | copy-start | bytes 12292
  663.8 37.9 %copy-start.7 = (s32[8]{0:T(128)S(1)}, s32[8]{0:T(128)}, u32[]{:S(2)}) copy-start(s32[8]{0:T(128)} %param.15) | copy-start | bytes 100
  663.8 38.1 %copy-start.9 = (f32[8,160]{1,0:T(8,128)S(1)}, f32[8,160]{1,0:T(8,128)}, u32[]{:S(2)}) copy-start(f32[8,160]{1,0:T(8,128)} %param.14) | copy-start | bytes 15364
  663.8 38.9 %copy-start.1 = (bf16[8192,128]{1,0:T(8,128)(2,1)S(1)}, bf16[8192,128]{1,0:T(8,128)(2,1)}, u32[]{:S(2)}) copy-start(bf16[8192,128]{1,0:T(8,128)(2,1)} %param.22) | copy-start | bytes 6291460
  685.5 11.7 %collective-permute-start.10 = (f32[160]{0:T(256)S(1)}, f32[160]{0:T(256)S(1)}, u32[]{:S(2)}, u32[]{:S(2)}) collective-permute-start(f32[160]{0:T(256)S(1)} %get-tuple-element.49), channel_id=1, source_target_pairs={{0,112},{4,116},{8,120},{12,124},{16,0},{20,4},{24,8},{28,12},{32,... | collective-permute-start | bytes 1928 | tf_op jit(solution)/shard_map/ppermute | solution.py:16
  685.5 11.7 %collective-permute-start.11 = (f32[160]{0:T(256)S(1)}, f32[160]{0:T(256)S(1)}, u32[]{:S(2)}, u32[]{:S(2)}) collective-permute-start(f32[160]{0:T(256)S(1)} %get-tuple-element.50), channel_id=1, source_target_pairs={{0,116},{4,120},{8,124},{12,0},{16,4},{20,8},{24,12},{28,16},{32,2... | collective-permute-start | bytes 1928 | tf_op jit(solution)/shard_map/ppermute | solution.py:16
  686.2 12.1 %collective-permute-start.12 = (f32[160]{0:T(256)S(1)}, f32[160]{0:T(256)S(1)}, u32[]{:S(2)}, u32[]{:S(2)}) collective-permute-start(f32[160]{0:T(256)S(1)} %get-tuple-element.51), channel_id=1, source_target_pairs={{0,120},{4,124},{8,0},{12,4},{16,8},{20,12},{24,16},{28,20},{32,24... | collective-permute-start | bytes 1928 | tf_op jit(solution)/shard_map/ppermute | solution.py:16
  695.2 3.1 collective-permute-start.13
  695.2 3.1 collective-permute-start.7
  697.2 3.6 collective-permute-start.8
  697.2 4.5 collective-permute-start.9
  701.8 0.9 copy-start.4
Sparse Core Ops, SparseCore 0:
  9.7 192.5 all-gather.1
where the time goes:
time: 718 us; the launch traced here: 710 us
  waiting for transfers between devices  511 us (71%)
  local copies, waits for them, and re-layouts  61.7 us (9%)
  matrix products  39.7 us (6%)
  between operations  34.9 us (5%)
  other arithmetic  32.1 us (4%)
  starting transfers between devices  23.6 us (3%)
    ppermute x14, waiting for transfers between devices, passed_along(): lax.ppermute(value, axis, [(i, (i + by) % length) for i in range(length)])  323 us
    all_gather x1, waiting for transfers between devices, local(): full_rows = lax.all_gather(hidden, 'mp', axis=1, tiled=True)  187 us
    gather x1, local copies, waits for them, and re-layouts, local(): packed = jnp.take(jnp.concatenate(received, axis=0), pick_rows, axis=0)  31.5 us
    ppermute x14, starting transfers between devices, passed_along(): lax.ppermute(value, axis, [(i, (i + by) % length) for i in range(length)])  23.6 us
    dot_general x1, matrix products, head_values(): jnp.einsum('hgqk,khd->qhgd', weights, value_rows, preferred_element_type=...  14.8 us
    dynamic_slice x1, local copies, waits for them, and re-layouts, outgoing(): lax.dynamic_slice_in_dim(source, slot_for(shift_by) * slot_rows, slot_row...  14.7 us
    dot_general x1, matrix products, local(): queries = jnp.dot(normed, w_query, preferred_element_type=jnp.float32)  14.4 us
  transfers between devices with their start and end apart: 15, of which 10 were waited for; matrix products, arithmetic and copies ran while one was open for 4% of the time, Pallas kernels for 0%

commit v1 on v0

--- a/solution.py
+++ b/solution.py
@@ -89,7 +89,11 @@
     row_offset = jnp.sum(jnp.where(lane_match, pack_offset[None, :], 0), axis=1)
     positions = jnp.arange(packed_rows, dtype=jnp.int32) - row_offset
     pick_rows = row_step * slot_rows + positions
-    full_rows = lax.all_gather(hidden, "mp", axis=1, tiled=True)
+    samples_drive = lambda shard_in, on_dim: jnp.concatenate(
+        lax.all_to_all(jnp.stack([shard_in for _ in range(lax.axis_size("mp"))], 0), "mp", 0, 0),
+        on_dim,
+    )
+    full_rows = samples_drive(hidden, on_dim=1)
     received = [outgoing(0, full_rows)]
     for shift_by in range(1, rollouts):
         received.append(passed_along(outgoing(shift_by, full_rows), "dp", shift_by))

time: 718 us -> 775 us (1.079)
  waiting for transfers between devices: 511 us -> 545 us
  local copies, waits for them, and re-layouts: 61.7 us -> 88.5 us
  between operations: 34.9 us -> 21.5 us
  starting transfers between devices: 23.6 us -> 33.3 us
    all_to_all x0 -> x1, waiting for transfers between devices: none -> 223 us  [local(): lax.all_to_all(jnp.stack([shard_in for _ in range(lax.axis_size('mp'))],...]
    all_gather x1 -> x0, waiting for transfers between devices: 187 us -> none  [local(): full_rows = lax.all_gather(hidden, 'mp', axis=1, tiled=True)]
    reshape x0 -> x1, local copies, waits for them, and re-layouts: none -> 17.5 us  [local(): jnp.concatenate(lax.all_to_all(jnp.stack([shard_in for _ in range(lax.axi...]
    another operation x0 -> x1, local copies, waits for them, and re-layouts: none -> 9.25 us  [local(): jnp.stack([shard_in for _ in range(lax.axis_size('mp'))], 0)]
    all_to_all x0 -> x1, starting transfers between devices: none -> 7.84 us  [local(): lax.all_to_all(jnp.stack([shard_in for _ in range(lax.axis_size('mp'))],...]
  transfers between devices with their start and end apart: 15 -> 15, of which waited for: 10 -> 11; matrix products, arithmetic and copies ran while one was open for 4% -> 3% of each run, Pallas kernels for 0% -> 0%
where the time goes in v1:
time: 775 us; the launch traced here: 766 us
  waiting for transfers between devices  545 us (70%)
  local copies, waits for them, and re-layouts  88.5 us (11%)
  matrix products  39.7 us (5%)
  starting transfers between devices  33.3 us (4%)
  other arithmetic  31.4 us (4%)
  between operations  21.5 us (3%)
    ppermute x14, waiting for transfers between devices, passed_along(): lax.ppermute(value, axis, [(i, (i + by) % length) for i in range(length)])  322 us
    all_to_all x1, waiting for transfers between devices, local(): lax.all_to_all(jnp.stack([shard_in for _ in range(lax.axis_size('mp'))],...  223 us
    gather x1, local copies, waits for them, and re-layouts, local(): packed = jnp.take(jnp.concatenate(received, axis=0), pick_rows, axis=0)  31.5 us
    ppermute x14, starting transfers between devices, passed_along(): lax.ppermute(value, axis, [(i, (i + by) % length) for i in range(length)])  25.4 us
    reshape x1, local copies, waits for them, and re-layouts, local(): jnp.concatenate(lax.all_to_all(jnp.stack([shard_in for _ in range(lax.axi...  17.5 us
  transfers between devices with their start and end apart: 15, of which 11 were waited for; matrix products, arithmetic and copies ran while one was open for 3% of the time, Pallas kernels for 0%

profile of v1, /device:TPU:1, one launch (start us, length us, event | category | flops | bytes accessed | tf_op | source)
XLA Modules:
  0.0 766.4 jit_solution(4902990976845659869)
XLA Ops:
  0.6 9.2 %stack.2 = bf16[4,1280,2048]{2,1,0:T(8,128)(2,1)} broadcast(bf16[1280,2048]{1,0:T(8,128)(2,1)} %param.13), dimensions={1,2} | broadcast | bytes 26214400 | tf_op jit(solution)/shard_map/stack | solution.py:93
  9.9 7.8 %all-to-all-start = ((bf16[4,1280,2048]{2,1,0:T(8,128)(2,1)}), bf16[4,1280,2048]{2,1,0:T(8,128)(2,1)}, u32[]{:S(2)}, u32[]{:S(2)}) async-start(bf16[4,1280,2048]{2,1,0:T(8,128)(2,1)} %stack.2), calls=%async_computation | async-start | bytes 41943040 | tf_op jit(solution)/shard_map/all_to_all | solution.py:93
  18.0 1.0 fusion.49
  24.1 222.7 %all-to-all-done = bf16[4,1280,2048]{2,1,0:T(8,128)(2,1)} async-done(((bf16[4,1280,2048]{2,1,0:T(8,128)(2,1)}), bf16[4,1280,2048]{2,1,0:T(8,128)(2,1)}, u32[]{:S(2)}, u32[]{:S(2)}) %all-to-all-start) | async-done | bytes 20971552 | tf_op jit(solution)/shard_map/all_to_all | solution.py:93
  246.8 17.5 %copy.42 = bf16[4,160,8,2048]{3,2,0,1:T(8,128)(2,1)} copy(bf16[4,160,8,2048]{3,2,1,0:T(8,128)(2,1)} %bitcast.14) | data formatting | bytes 41943040 | tf_op jit(solution)/shard_map/reshape | solution.py:92
  264.3 14.7 %constant_dynamic-slice_fusion = (bf16[160,8192]{1,0:T(8,128)(2,1)}, bf16[160,8192]{1,0:T(8,128)(2,1)}, bf16[160,8192]{1,0:T(8,128)(2,1)}, bf16[160,8192]{1,0:T(...) fusion(bf16[1280,8192]{1,0:T(8,128)(2,1)} %bitcast.53, ...), kind=kLoop, calls=%fused_computation.95 | loop fusion | bytes 41943072 | tf_op jit(solution)/shard_map/dynamic_slice | solution.py:84
  279.0 2.6 collective-permute-start
  281.6 5.7 fusion.58
  302.4 0.7 iota_compare_fusion.10
  303.1 1.3 collective-permute-start.1
  304.4 0.7 iota_compare_fusion.3
  305.6 0.7 iota_compare_fusion.5
  306.3 0.6 iota_compare_fusion.6
  307.0 0.7 iota_compare_fusion.7
  307.7 1.6 collective-permute-start.2
  309.7 1.2 multiply_cosine_fusion
  310.9 1.9 collective-permute-start.3
  312.8 3.4 collective-permute-start.4
  316.4 2.8 collective-permute-start.5
  319.3 3.5 constant_dynamic-update-slice_fusion.6
  322.8 52.9 %collective-permute-done.1 = bf16[160,8192]{1,0:T(8,128)(2,1)S(1)} collective-permute-done((bf16[160,8192]{1,0:T(8,128)(2,1)}, bf16[160,8192]{1,0:T(8,128)(2,1)S(1)}, u32[]{:S(2)}, u32[]{:S(2)}) %collective-permute-start.1) | collective-permute-done | bytes 2621472 | tf_op jit(solution)/shard_map/ppermute | solution.py:16
  375.6 1.7 constant_dynamic-update-slice_fusion.5
  377.4 51.4 %collective-permute-done.2 = bf16[160,8192]{1,0:T(8,128)(2,1)S(1)} collective-permute-done((bf16[160,8192]{1,0:T(8,128)(2,1)}, bf16[160,8192]{1,0:T(8,128)(2,1)S(1)}, u32[]{:S(2)}, u32[]{:S(2)}) %collective-permute-start.2) | collective-permute-done | bytes 2621472 | tf_op jit(solution)/shard_map/ppermute | solution.py:16
  428.8 1.8 constant_dynamic-update-slice_fusion.4
  430.6 101.0 %collective-permute-done.3 = bf16[160,8192]{1,0:T(8,128)(2,1)S(1)} collective-permute-done((bf16[160,8192]{1,0:T(8,128)(2,1)}, bf16[160,8192]{1,0:T(8,128)(2,1)S(1)}, u32[]{:S(2)}, u32[]{:S(2)}) %collective-permute-start.3) | collective-permute-done | bytes 2621472 | tf_op jit(solution)/shard_map/ppermute | solution.py:16
  531.6 1.7 constant_dynamic-update-slice_fusion.3
  533.3 33.6 %collective-permute-done.4 = bf16[160,8192]{1,0:T(8,128)(2,1)S(1)} collective-permute-done((bf16[160,8192]{1,0:T(8,128)(2,1)}, bf16[160,8192]{1,0:T(8,128)(2,1)S(1)}, u32[]{:S(2)}, u32[]{:S(2)}) %collective-permute-start.4) | collective-permute-done | bytes 2621472 | tf_op jit(solution)/shard_map/ppermute | solution.py:16
  566.9 1.7 constant_dynamic-update-slice_fusion.2
  568.6 53.1 %collective-permute-done.5 = bf16[160,8192]{1,0:T(8,128)(2,1)S(1)} collective-permute-done((bf16[160,8192]{1,0:T(8,128)(2,1)}, bf16[160,8192]{1,0:T(8,128)(2,1)S(1)}, u32[]{:S(2)}, u32[]{:S(2)}) %collective-permute-start.5) | collective-permute-done | bytes 2621472 | tf_op jit(solution)/shard_map/ppermute | solution.py:16
  621.7 1.7 constant_dynamic-update-slice_fusion.1
  623.4 26.7 %collective-permute-done.6 = bf16[160,8192]{1,0:T(8,128)(2,1)S(1)} collective-permute-done((bf16[160,8192]{1,0:T(8,128)(2,1)}, bf16[160,8192]{1,0:T(8,128)(2,1)S(1)}, u32[]{:S(2)}, u32[]{:S(2)}) %collective-permute-start.6) | collective-permute-done | bytes 2621472 | tf_op jit(solution)/shard_map/ppermute | solution.py:16
  650.1 1.7 constant_dynamic-update-slice_fusion
  651.8 31.5 %gather_fusion = bf16[640,8192]{1,0:T(8,128)(2,1)} fusion(bf16[1280,8192]{1,0:T(8,128)(2,1)} %constant_dynamic-update-slice_fusion, s32[1024]{0:T(1024)S(1)} %pad_clamp_fusion), kind=kCustom, calls=%fused_computation | custom fusion | bytes 20974080 | tf_op jit(solution)/shard_map/jit(_take)/gather | solution.py:100
  683.3 7.7 %fusion = (f32[640]{0:T(1024)S(1)}, bf16[640,8192]{1,0:T(8,128)(2,1)S(1)}) fusion(bf16[640,8192]{1,0:T(8,128)(2,1)} %gather_fusion, pred[640]{0:T(1024)(128)(4,1)S(1)} %compare_and_fusion.1), kind=kLoop, calls=%fused_computation.3 | loop fusion | flops 20970880 | bytes 20974720 | tf_op jit(solution)/shard_map/reduce_sum | solution.py:102
  691.0 3.3 convolution_bitcast_fusion.1
  694.3 0.7 fusion.36
  695.0 14.4 %convolution_bitcast_fusion = f32[80,8,8,128]{3,1,2,0:T(8,128)S(1)} fusion(bf16[8192,1024]{1,0:T(8,128)(2,1)} %param.21, bf16[640,8192]{1,0:T(8,128)(2,1)S(1)} %get-tuple-element.29, f32[8192]{0:T(1024)S(1)} %copy-done.10, f32[640]{0:T(1024)S(1)} %add_rsqrt_fusion), kind=kOutput, calls=%fused_computation.20 | convolution fusion | flops 10758389760 | bytes 29919744 | tf_op jit(solution)/shard_map/dot_general | solution.py:104
  710.0 0.8 fusion.86
  710.8 1.0 subtract_convert_fusion
  711.8 6.4 fusion.3
  718.2 7.8 %fusion.4 = f32[8,640]{1,0:T(8,128)S(1)} fusion(f32[640,640,8]{1,0,2:T(8,128)} %get-tuple-element.58, f32[8,640]{1,0:T(8,128)S(1)} %get-tuple-element.57, pred[640,640]{0,1:T(8,128)(4,1)S(1)} %compare_and_fusion), kind=kLoop, calls=%fused_computation.11 | loop fusion | flops 16378880 | bytes 13557760 | tf_op jit(solution)/shard_map/reduce_sum | solution.py:50
  726.7 14.8 %fusion.7 = f32[640]{0:T(1024)S(1)} fusion(f32[8,640]{1,0:T(8,128)S(1)} %fusion.4, f32[8,640]{1,0:T(8,128)S(1)} %get-tuple-element.57, f32[640,640,8]{1,0,2:T(8,128)} %get-tuple-element.58, pred[640,640]{0,1:T(8,128)(4,1)S(1)} %compare_and_fusion, f32[8,128]{1,0:T(8,128)S(1)} %bitcast.55, bf16[8192,128]{1,0:T(8,128)(2,1)} %param.23, ...), kind=kOutput, calls=%fused_computation.16 | convolution fusion | flops 2223062528 | bytes 26182656 | tf_op jit(solution)/shard_map/hgqk,khd->qhgd/dot_general | solution.py:52
  741.6 6.9 psum.7
  749.3 9.7 %collective-permute-start.12 = (f32[160]{0:T(256)S(1)}, f32[160]{0:T(256)S(1)}, u32[]{:S(2)}, u32[]{:S(2)}) collective-permute-start(f32[160]{0:T(256)S(1)} %get-tuple-element.51), channel_id=1, source_target_pairs={{0,120},{4,124},{8,0},{12,4},{16,8},{20,12},{24,16},{28,20},{32,24... | collective-permute-start | bytes 1928 | tf_op jit(solution)/shard_map/ppermute | solution.py:16
  759.1 1.6 collective-permute-start.7
  762.1 2.2 collective-permute-done.8
  764.3 0.9 collective-permute-done.9
  765.3 0.8 fusion.25
  (57 shorter events, 5.0 us)
Async XLA Ops:
  0.6 690.3 %copy-start = (bf16[8192,128]{1,0:T(8,128)(2,1)S(1)}, bf16[8192,128]{1,0:T(8,128)(2,1)}, u32[]{:S(2)}) copy-start(bf16[8192,128]{1,0:T(8,128)(2,1)} %param.22) | copy-start | bytes 6291460
  9.9 8.1 %copy-start.7 = (s32[8]{0:T(128)S(1)}, s32[8]{0:T(128)}, u32[]{:S(2)}) copy-start(s32[8]{0:T(128)} %param.16) | copy-start | bytes 100
  9.9 8.1 %copy-start.8 = (s32[8]{0:T(128)S(1)}, s32[8]{0:T(128)}, u32[]{:S(2)}) copy-start(s32[8]{0:T(128)} %param.17) | copy-start | bytes 100
  9.9 236.8 %all-to-all-start = ((bf16[4,1280,2048]{2,1,0:T(8,128)(2,1)}), bf16[4,1280,2048]{2,1,0:T(8,128)(2,1)}, u32[]{:S(2)}, u32[]{:S(2)}) async-start(bf16[4,1280,2048]{2,1,0:T(8,128)(2,1)} %stack.2), calls=%async_computation | async-start | bytes 41943040 | tf_op jit(solution)/shard_map/all_to_all | solution.py:93
  264.3 17.3 %copy-start.6 = (s32[8]{0:T(128)S(1)}, s32[8]{0:T(128)}, u32[]{:S(2)}) copy-start(s32[8]{0:T(128)} %param.18) | copy-start | bytes 100
  264.3 38.0 %copy-start.3 = (s32[640]{0:T(1024)S(1)}, s32[640]{0:T(1024)}, u32[]{:S(2)}) copy-start(s32[640]{0:T(1024)} %param.19) | copy-start | bytes 7684
  279.0 37.4 %collective-permute-start = (bf16[160,8192]{1,0:T(8,128)(2,1)}, bf16[160,8192]{1,0:T(8,128)(2,1)}, u32[]{:S(2)}, u32[]{:S(2)}) collective-permute-start(bf16[160,8192]{1,0:T(8,128)(2,1)} %get-tuple-element.36), channel_id=1, source_target_pairs={{0,4},{4,8},{8,12},{12,16},{16,20},{20,24},{24,28},{28,32},{32,36}... | collective-permute-start | bytes 7864328 | tf_op jit(solution)/shard_map/ppermute | solution.py:16
  303.1 72.6 %collective-permute-start.1 = (bf16[160,8192]{1,0:T(8,128)(2,1)}, bf16[160,8192]{1,0:T(8,128)(2,1)S(1)}, u32[]{:S(2)}, u32[]{:S(2)}) collective-permute-start(bf16[160,8192]{1,0:T(8,128)(2,1)} %get-tuple-element.35), channel_id=1, source_target_pairs={{0,8},{4,12},{8,16},{12,20},{16,24},{20,28},{24,32},{28,36},{32,40... | collective-permute-start | bytes 7864328 | tf_op jit(solution)/shard_map/ppermute | solution.py:16
  307.7 121.1 %collective-permute-start.2 = (bf16[160,8192]{1,0:T(8,128)(2,1)}, bf16[160,8192]{1,0:T(8,128)(2,1)S(1)}, u32[]{:S(2)}, u32[]{:S(2)}) collective-permute-start(bf16[160,8192]{1,0:T(8,128)(2,1)} %get-tuple-element.34), channel_id=1, source_target_pairs={{0,12},{4,16},{8,20},{12,24},{16,28},{20,32},{24,36},{28,40},{32,4... | collective-permute-start | bytes 7864328 | tf_op jit(solution)/shard_map/ppermute | solution.py:16
  310.9 220.7 %collective-permute-start.3 = (bf16[160,8192]{1,0:T(8,128)(2,1)}, bf16[160,8192]{1,0:T(8,128)(2,1)S(1)}, u32[]{:S(2)}, u32[]{:S(2)}) collective-permute-start(bf16[160,8192]{1,0:T(8,128)(2,1)} %get-tuple-element.33), channel_id=1, source_target_pairs={{0,16},{4,20},{8,24},{12,28},{16,32},{20,36},{24,40},{28,44},{32,4... | collective-permute-start | bytes 7864328 | tf_op jit(solution)/shard_map/ppermute | solution.py:16
  312.8 254.1 %collective-permute-start.4 = (bf16[160,8192]{1,0:T(8,128)(2,1)}, bf16[160,8192]{1,0:T(8,128)(2,1)S(1)}, u32[]{:S(2)}, u32[]{:S(2)}) collective-permute-start(bf16[160,8192]{1,0:T(8,128)(2,1)} %get-tuple-element.32), channel_id=1, source_target_pairs={{0,20},{4,24},{8,28},{12,32},{16,36},{20,40},{24,44},{28,48},{32,5... | collective-permute-start | bytes 7864328 | tf_op jit(solution)/shard_map/ppermute | solution.py:16
  316.4 305.3 %collective-permute-start.5 = (bf16[160,8192]{1,0:T(8,128)(2,1)}, bf16[160,8192]{1,0:T(8,128)(2,1)S(1)}, u32[]{:S(2)}, u32[]{:S(2)}) collective-permute-start(bf16[160,8192]{1,0:T(8,128)(2,1)} %get-tuple-element.31), channel_id=1, source_target_pairs={{0,24},{4,28},{8,32},{12,36},{16,40},{20,44},{24,48},{28,52},{32,5... | collective-permute-start | bytes 7864328 | tf_op jit(solution)/shard_map/ppermute | solution.py:16
  375.6 274.5 %collective-permute-start.6 = (bf16[160,8192]{1,0:T(8,128)(2,1)}, bf16[160,8192]{1,0:T(8,128)(2,1)S(1)}, u32[]{:S(2)}, u32[]{:S(2)}) collective-permute-start(bf16[160,8192]{1,0:T(8,128)(2,1)} %get-tuple-element.30), channel_id=1, source_target_pairs={{0,28},{4,32},{8,36},{12,40},{16,44},{20,48},{24,52},{28,56},{32,6... | collective-permute-start | bytes 7864328 | tf_op jit(solution)/shard_map/ppermute | solution.py:16
  683.3 7.7 %copy-start.10 = (f32[8192]{0:T(1024)S(1)}, f32[8192]{0:T(1024)}, u32[]{:S(2)}) copy-start(f32[8192]{0:T(1024)} %param.20) | copy-start | bytes 98308
  691.0 35.1 %copy-start.2 = (bf16[640,8192]{1,0:T(8,128)(2,1)}, bf16[640,8192]{1,0:T(8,128)(2,1)S(1)}, u32[]{:S(2)}) copy-start(bf16[640,8192]{1,0:T(8,128)(2,1)S(1)} %get-tuple-element.29) | copy-start | bytes 31457284
  718.2 7.9 %copy-start.5 = (f32[2048]{0:T(1024)S(1)}, f32[2048]{0:T(1024)}, u32[]{:S(2)}) copy-start(f32[2048]{0:T(1024)} %param.24) | copy-start | bytes 24580
  718.2 8.5 %copy-start.12 = (f32[1024]{0:T(1024)S(1)}, f32[1024]{0:T(1024)}, u32[]{:S(2)}) copy-start(f32[1024]{0:T(1024)} %param.25) | copy-start | bytes 12292
  726.7 38.4 %copy-start.9 = (s32[8]{0:T(128)S(1)}, s32[8]{0:T(128)}, u32[]{:S(2)}) copy-start(s32[8]{0:T(128)} %param.15) | copy-start | bytes 100
  726.7 38.6 %copy-start.11 = (f32[8,160]{1,0:T(8,128)S(1)}, f32[8,160]{1,0:T(8,128)}, u32[]{:S(2)}) copy-start(f32[8,160]{1,0:T(8,128)} %param.14) | copy-start | bytes 15364
  726.7 39.4 %copy-start.1 = (bf16[8192,128]{1,0:T(8,128)(2,1)S(1)}, bf16[8192,128]{1,0:T(8,128)(2,1)}, u32[]{:S(2)}) copy-start(bf16[8192,128]{1,0:T(8,128)(2,1)} %param.22) | copy-start | bytes 6291460
  748.6 12.1 %collective-permute-start.10 = (f32[160]{0:T(256)S(1)}, f32[160]{0:T(256)S(1)}, u32[]{:S(2)}, u32[]{:S(2)}) collective-permute-start(f32[160]{0:T(256)S(1)} %get-tuple-element.49), channel_id=1, source_target_pairs={{0,112},{4,116},{8,120},{12,124},{16,0},{20,4},{24,8},{28,12},{32,... | collective-permute-start | bytes 1928 | tf_op jit(solution)/shard_map/ppermute | solution.py:16
  748.6 12.0 %collective-permute-start.11 = (f32[160]{0:T(256)S(1)}, f32[160]{0:T(256)S(1)}, u32[]{:S(2)}, u32[]{:S(2)}) collective-permute-start(f32[160]{0:T(256)S(1)} %get-tuple-element.50), channel_id=1, source_target_pairs={{0,116},{4,120},{8,124},{12,0},{16,4},{20,8},{24,12},{28,16},{32,2... | collective-permute-start | bytes 1928 | tf_op jit(solution)/shard_map/ppermute | solution.py:16
  749.3 12.3 %collective-permute-start.12 = (f32[160]{0:T(256)S(1)}, f32[160]{0:T(256)S(1)}, u32[]{:S(2)}, u32[]{:S(2)}) collective-permute-start(f32[160]{0:T(256)S(1)} %get-tuple-element.51), channel_id=1, source_target_pairs={{0,120},{4,124},{8,0},{12,4},{16,8},{20,12},{24,16},{28,20},{32,24... | collective-permute-start | bytes 1928 | tf_op jit(solution)/shard_map/ppermute | solution.py:16
  759.1 3.0 collective-permute-start.13
  759.1 3.0 collective-permute-start.7
  760.6 3.6 collective-permute-start.8
  760.6 4.5 collective-permute-start.9
  765.2 0.9 copy-start.4
